TPU v7x, 128 devices: a whole 4x4x4 slice. The times are simulated.
128 devices in a mesh: lat: 16 (over x, y_lo, core), lon: 8 (over z, y_hi).
Axes of the slice: x: 4, y: 4 (y_hi: 2, y_lo: 2; y = y_hi * 2 + y_lo), z: 4, core: 2. Of those that a mesh axis runs over, the one named last changes fastest.
Arguments:
- field: bfloat16 [256, 16384], P('lat', 'lon'), may hold values from -6 to 6
- stored_row: int32 [256], replicated, may hold values from 0 to 255, as said below
- row_len: int32 [256], replicated, may hold values from 1537 to 2048
- offset: int32 [256], replicated, may hold values from -2 to 1
- first_weight: bfloat16 [32, 9], replicated, may hold values from -2 to 2
- first_bias: float32 [32], replicated, may hold values from -3 to 3
- second_weight: bfloat16 [64, 288], replicated, may hold values from -0.375 to 0.375
- second_bias: float32 [64], replicated, may hold values from -3 to 3
Outputs:
- pooled: bfloat16 [64, 128, 8192], P(None, 'lat', 'lon')
Inputs may be any that keep to these rules, and one draw needn't show every extreme that they name: stored_row is a permutation; the 16 slots of one lat device hold rows of exactly 8 tiles of 16 consecutive rows, 2 rows of each.
All inputs are finite; a program needn't handle non-finite values.
Results may differ from a plain program's by a relative error of at most 0.0031.
The roundings to bfloat16 on the way count: a program that leaves them out, or rounds other values in their place, can miss the bound.
Values may be sent and summed in bfloat16 or wider, within the bound.
A program may use at most 128 MiB of HBM per device.

v0:
```python
import jax
import jax.numpy as jnp
from jax import lax
from jax.sharding import PartitionSpec as P

Q = 2048
GROUPS = 8
D1 = 2
D2 = 8


def with_halo(block, sides, width):
    for axis, dim in sides:
        count = lax.axis_size(axis)
        forward = [(i, i + 1) for i in range(count - 1)]
        forward.append((count - 1, 0))
        backward = [(target, source) for source, target in forward]
        low = lax.ppermute(
            lax.slice_in_dim(block, block.shape[dim] - width, None, axis=dim), axis, forward
        )
        high = lax.ppermute(lax.slice_in_dim(block, 0, width, axis=dim), axis, backward)
        block = jnp.concatenate([low, block, high], axis=dim)
    return block


def resample(source, prev_tail, next_head, lengths, offsets, columns):
    index_q = jnp.arange(columns, dtype=jnp.int32)
    length_f = lengths.astype(jnp.float32)[..., None]
    position = (
        (2 * index_q + 1).astype(jnp.float32) * length_f / (2.0 * columns)
        - 0.5
        - 0.25 * offsets.astype(jnp.float32)[..., None]
    )
    floored = jnp.floor(position)
    weight = position - floored
    lower_index = floored.astype(jnp.int32)
    last_slot = source.shape[-1] - 1

    def point_value(index):
        inside = jnp.take_along_axis(source, jnp.clip(index, 0, last_slot), axis=-1).astype(
            jnp.float32
        )
        picked = jnp.where(index < 0, prev_tail[..., None].astype(jnp.float32), inside)
        return jnp.where(
            index >= lengths[..., None], next_head[..., None].astype(jnp.float32), picked
        )

    return (
        (1.0 - weight) * point_value(lower_index) + weight * point_value(lower_index + 1)
    ).astype(jnp.bfloat16)


def keep_rows(values, first_row, row_total):
    count_rows = values.shape[-2]
    global_rows = first_row + jnp.arange(count_rows, dtype=jnp.int32)
    kept_mask = (global_rows >= 0) & (global_rows < row_total)
    return jnp.where(kept_mask[:, None], values, jnp.zeros((), values.dtype))


def first_layer(padded, first_weight, first_bias, dilation):
    kernel = first_weight.reshape(first_weight.shape[0], 1, 3, 3)
    summed = lax.conv_general_dilated(
        padded[None, None],
        kernel,
        (1, 1),
        "VALID",
        rhs_dilation=(dilation, dilation),
        dimension_numbers=("NCHW", "OIHW", "NCHW"),
        preferred_element_type=jnp.float32,
    )[0]
    return jax.nn.gelu(summed + first_bias[:, None, None]).astype(jnp.bfloat16)


def second_layer(hidden, second_weight, second_bias, dilation, out_rows):
    channels = hidden.shape[0]
    outputs = second_weight.shape[0]
    kernel = second_weight.reshape(outputs, 3, 3, channels).transpose(0, 3, 1, 2)
    summed = lax.conv_general_dilated(
        hidden[None],
        kernel,
        (1, 1),
        "VALID",
        rhs_dilation=(dilation, dilation),
        dimension_numbers=("NCHW", "OIHW", "NCHW"),
        preferred_element_type=jnp.float32,
    )[0]
    active = jax.nn.gelu(summed + second_bias[:, None, None])
    out_cols = active.shape[2]
    return (
        active.reshape(outputs, out_rows // 2, 2, out_cols // 2, 2)
        .mean(axis=(2, 4))
        .astype(jnp.bfloat16)
    )


def interpolate(source, row_ids, row_len, offset):
    lengths = jnp.take(row_len, row_ids)
    shifts = jnp.take(offset, row_ids)
    last_point = jnp.take_along_axis(source, (lengths - 1)[:, None], axis=1)[:, 0]
    edge_pair = jnp.stack([source[:, 0], last_point], axis=1)
    beside_edges = with_halo(edge_pair, (("lon", 1),), 1)
    return resample(source, beside_edges[:, 0], beside_edges[:, 3], lengths, shifts, Q)


def pack_rows(values, stored_row, lat_index, band_count, capacity):
    row_count = values.shape[0]
    held_ids = lax.dynamic_slice_in_dim(stored_row, lat_index * row_count, row_count)
    tile_of = held_ids // row_count
    one_hot = (tile_of[:, None] == jnp.arange(band_count, dtype=jnp.int32)[None, :]).astype(
        jnp.int32
    )
    rank_of = jnp.sum((jnp.cumsum(one_hot, axis=0) - 1) * one_hot, axis=1)
    slot_of = tile_of * capacity + rank_of
    buffer = (
        jnp.zeros((band_count * capacity, values.shape[1]), values.dtype).at[slot_of].set(values)
    )
    return buffer.reshape(band_count, capacity, values.shape[1])


def unpack_rows(arrived, stored_row, lat_index, row_count, band_count, capacity):
    held_all = stored_row.reshape(band_count, row_count)
    tile_of = held_all // row_count
    one_hot = (
        tile_of[:, :, None] == jnp.arange(band_count, dtype=jnp.int32)[None, None, :]
    ).astype(jnp.int32)
    rank_of = jnp.sum((jnp.cumsum(one_hot, axis=1) - 1) * one_hot, axis=2)
    slot_of = jnp.arange(band_count, dtype=jnp.int32)[:, None] * capacity + rank_of
    is_mine = tile_of == lat_index
    target = jnp.where(is_mine, held_all % row_count, row_count)
    source = (
        jnp.zeros((row_count,), jnp.int32)
        .at[target.reshape(-1)]
        .set(slot_of.reshape(-1), mode="drop")
    )
    flat_rows = arrived.reshape(band_count * capacity, arrived.shape[2])
    return jnp.take(flat_rows, source, axis=0)


def per_device(
    field, stored_row, row_len, offset, first_weight, first_bias, second_weight, second_bias
):
    row_count = field.shape[0]
    band_count = lax.axis_size("lat")
    lat_index = lax.axis_index("lat")
    row_total = row_count * band_count
    capacity = row_count // GROUPS
    bundle = pack_rows(field, stored_row, lat_index, band_count, capacity)
    arrived = lax.all_to_all(bundle, "lat", split_axis=0, concat_axis=0, tiled=True)
    tiled_rows = unpack_rows(arrived, stored_row, lat_index, row_count, band_count, capacity)
    row_ids = lat_index * row_count + jnp.arange(row_count, dtype=jnp.int32)
    regular = interpolate(tiled_rows, row_ids, row_len, offset)
    border = with_halo(regular, (("lat", 0), ("lon", 1)), D1 + D2)
    border = keep_rows(border, lat_index * row_count - D1 - D2, row_total)
    hidden = keep_rows(
        first_layer(border, first_weight, first_bias, D1), lat_index * row_count - D2, row_total
    )
    return second_layer(hidden, second_weight, second_bias, D2, row_count)


def solution(mesh):
    placed = (P("lat", "lon"), P(), P(), P(), P(), P(), P(), P())
    return jax.shard_map(
        per_device, mesh=mesh, in_specs=placed, out_specs=P(None, "lat", "lon"), check_vma=False
    )
```

profile of v0, /device:TPU:1, one launch (start us, length us, event | category | flops | bytes accessed | tf_op | source)
XLA Modules:
  0.0 746.4 jit_solution(12020246102050681139)
XLA Ops:
  0.0 0.8 and_select_fusion.3
  0.9 0.2 select_reduce_fusion
  1.1 0.8 compare_select_fusion.5
  1.8 1.0 scatter_custom_fusion.1
  2.9 0.8 reshape.181
  3.6 6.8 all-to-all-start
  10.5 0.7 compare_select_fusion.2
  11.2 0.8 reshape.180
  12.0 0.5 fusion.53
  12.6 0.1 reshape.251
  12.7 1.4 scatter_custom_fusion
  14.1 0.7 gather_fusion.3
  14.8 1.3 gather_fusion.2
  16.2 0.2 fusion.29
  16.5 0.1 all-to-all-done
  16.7 0.6 gather_fusion
  17.3 0.1 broadcast_select_fusion
  17.4 0.7 gather_fusion.1
  18.1 2.7 collective-permute-start.1
  20.8 3.6 collective-permute-start
  24.3 274.7 %gather_fusion.5 = bf16[32768]{0:T(1024)(128)(2,1)S(1)} fusion(bf16[16,2048]{1,0:T(8,128)(2,1)S(1)} %broadcast_select_fusion, s32[32768]{0:T(1024)S(1)} %bitcast.58), kind=kCustom, calls=%fused_computation.3.clone | custom fusion | bytes 393216 | tf_op jit(solution)/shard_map/jit(take_along_axis)/gather | solution.py:40
  299.2 274.7 %gather_fusion.4 = bf16[32768]{0:T(1024)(128)(2,1)S(1)} fusion(bf16[16,2048]{1,0:T(8,128)(2,1)S(1)} %broadcast_select_fusion, s32[32768]{0:T(1024)S(1)} %bitcast.57), kind=kCustom, calls=%fused_computation.1.clone | custom fusion | bytes 393216 | tf_op jit(solution)/shard_map/jit(take_along_axis)/gather | solution.py:40
  574.0 0.1 convert_reduce_fusion
  574.1 0.3 add_convert_fusion
  574.4 1.3 collective-permute-start.2
  575.7 0.1 copy.56
  575.8 1.2 collective-permute-done.2
  577.0 2.7 collective-permute-done.3
  579.7 0.1 fusion.51
  579.8 4.2 collective-permute-start.5
  584.0 0.8 collective-permute-done.5
  584.8 5.3 collective-permute-done.4
  590.1 0.2 concatenate.23
  590.3 0.1 select_bitcast_fusion.1
  590.4 0.3 reshape.188
  590.7 0.1 fusion.28
  590.8 8.6 %copy.54 = bf16[1,36,8,263]{2,0,3,1:T(2,128)(2,1)} copy(bf16[1,36,8,263]{3,2,1,0:T(8,128)(2,1)S(1)} %fusion.28) | data formatting | bytes 302976 | tf_op jit(solution)/shard_map/conv_general_dilated | solution.py:62
  599.4 38.4 %select_bitcast_fusion = bf16[32,1,8,259,32]{4,2,3,0,1:T(8,128)(2,1)S(1)} fusion(f32[32]{0:T(128)S(1)} %copy-done.6, pred[32]{0:T(512)(128)(4,1)S(1)} %compare_and_fusion.3, pred[8,259]{0,1:T(8,128)(4,1)S(1)} %copy-done.7, bf16[1,36,8,263]{2,0,3,1:T(2,128)(2,1)} %copy.54, bf16[32,1,3,3]{0,1,3,2:T(2,128)(2,1)S(1)} %reshape.293), kind=kOutput, calls=%fused_computation.25 | convolution fusion | flops 65773568 | bytes 4397752 | tf_op jit(solution)/shard_map/conv_general_dilated | solution.py:62
  637.8 5.8 copy-done.2
  643.6 0.3 slice.41
  643.9 31.4 %fusion.11 = f32[16,8,259,64]{3,1,2,0:T(8,128)} fusion(bf16[64,3,3,32]{0,3,2,1:T(8,128)(2,1)S(1)} %bitcast.60, bf16[32,1,7,16,32]{4,2,3,0,1:T(8,128)(2,1)S(1)} %slice.41, bf16[32,1,8,259,32]{4,2,3,0,1:T(8,128)(2,1)} %copy-done.2), kind=kOutput, calls=%fused_computation.21 | convolution fusion | flops 1235632128 | bytes 12996608 | tf_op jit(solution)/shard_map/conv_general_dilated | solution.py:78
  675.3 15.6 %copy.57 = f32[16,8,259,64]{2,1,3,0:T(8,128)} copy(f32[16,8,259,64]{3,1,2,0:T(8,128)} %fusion.11) | data formatting | bytes 16973824 | tf_op jit(solution)/shard_map/conv_general_dilated | solution.py:78
  691.0 12.4 %reshape.195 = f32[16,1,2072,64]{2,3,0,1:T(8,128)} reshape(f32[16,8,259,64]{2,1,3,0:T(8,128)} %copy.57) | data formatting | bytes 16973824 | tf_op jit(solution)/shard_map/conv_general_dilated | solution.py:78
  703.4 7.7 %slice_bitcast_fusion = f32[1,64,16,2048]{3,1,2,0:T(8,128)} fusion(f32[16,1,2072,64]{2,3,0,1:T(8,128)} %reshape.195), kind=kLoop, calls=%fused_computation.36 | loop fusion | bytes 16777216 | tf_op jit(solution)/shard_map/conv_general_dilated | solution.py:78
  711.1 12.2 %copy.58 = f32[1,64,16,2048]{1,3,2,0:T(8,128)} copy(f32[1,64,16,2048]{3,1,2,0:T(8,128)} %slice_bitcast_fusion) | data formatting | bytes 16777216 | tf_op jit(solution)/shard_map/conv_general_dilated | solution.py:78
  723.3 16.1 %copy.59 = f32[64,8,2,1024,2]{3,1,4,2,0:T(8,128)} copy(f32[64,8,2,1024,2]{0,4,3,2,1:T(2,128)} %bitcast.59) | data formatting | bytes 16777216 | tf_op jit(solution)/shard_map/squeeze | solution.py:78
  739.5 5.7 fusion.24
  745.2 1.2 multiply_convert_fusion
  (54 shorter events, 0.8 us)
Async XLA Ops:
  0.0 14.1 %copy-start = (s32[256]{0:T(256)S(1)}, s32[256]{0:T(256)}, u32[]{:S(2)}) copy-start(s32[256]{0:T(256)} %param.15) | copy-start | bytes 3076
  3.6 13.0 %all-to-all-start = ((bf16[16,2,2048]{2,1,0:T(2,128)(2,1)}), bf16[16,2,2048]{2,1,0:T(2,128)(2,1)S(1)}, u32[]{:S(2)}, u32[]{:S(2)}) async-start(bf16[16,2,2048]{2,1,0:T(2,128)(2,1)} %reshape.181), calls=%async_computation | async-start | bytes 262144 | tf_op jit(solution)/shard_map/all_to_all | solution.py:148
  18.1 555.8 %collective-permute-start.1 = (bf16[16,1]{0,1:T(2,128)(2,1)S(1)}, bf16[16,1]{0,1:T(2,128)(2,1)S(1)}, u32[]{:S(2)}, u32[]{:S(2)}) collective-permute-start(bf16[16,1]{0,1:T(2,128)(2,1)S(1)} %fusion.44), channel_id=1, source_target_pairs={{0,1},{1,2},{2,3},{3,4},{4,5},{5,6},{6,7},{7,0},{8,9},{9,10},{10,1... | collective-permute-start | bytes 104 | tf_op jit(solution)/shard_map/ppermute | solution.py:18
  20.8 553.2 %collective-permute-start = (bf16[16,1]{1,0:T(8,128)(2,1)S(1)}, bf16[16,1]{1,0:T(8,128)(2,1)S(1)}, u32[]{:S(2)}, u32[]{:S(2)}) collective-permute-start(bf16[16,1]{1,0:T(8,128)(2,1)S(1)} %slice.35), channel_id=1, source_target_pairs={{1,0},{2,1},{3,2},{4,3},{5,4},{6,5},{7,6},{0,7},{9,8},{10,9},{11,1... | collective-permute-start | bytes 104 | tf_op jit(solution)/shard_map/ppermute | solution.py:21
  299.1 276.6 %copy-start.4 = (bf16[32,9]{0,1:T(8,128)(2,1)S(1)}, bf16[32,9]{0,1:T(8,128)(2,1)}, u32[]{:S(2)}) copy-start(bf16[32,9]{0,1:T(8,128)(2,1)} %param.16) | copy-start | bytes 1732
  299.1 276.6 %copy-start.3 = (bf16[64,288]{1,0:T(8,128)(2,1)S(1)}, bf16[64,288]{1,0:T(8,128)(2,1)}, u32[]{:S(2)}) copy-start(bf16[64,288]{1,0:T(8,128)(2,1)} %param.18) | copy-start | bytes 110596
  299.1 300.3 %copy-start.6 = (f32[32]{0:T(128)S(1)}, f32[32]{0:T(128)}, u32[]{:S(2)}) copy-start(f32[32]{0:T(128)} %param.17) | copy-start | bytes 388
  299.1 300.3 %copy-start.7 = (pred[8,259]{0,1:T(8,128)(4,1)S(1)}, pred[8,259]{0,1:T(8,128)(4,1)}, u32[]{:S(2)}) copy-start(pred[8,259]{0,1:T(8,128)(4,1)} %constant.168) | copy-start | bytes 6220
  574.4 2.6 collective-permute-start.2
  575.7 4.0 collective-permute-start.3
  579.8 5.0 collective-permute-start.5
  584.0 6.1 collective-permute-start.4
  637.8 5.8 copy-start.2
  723.3 16.1 %copy-start.5 = (f32[64]{0:T(128)S(1)}, f32[64]{0:T(128)}, u32[]{:S(2)}) copy-start(f32[64]{0:T(128)} %param.19) | copy-start | bytes 772
  723.3 23.1 %copy-start.1 = (s32[256]{0:T(256)S(1)}, s32[256]{0:T(256)}, u32[]{:S(2)}) copy-start(s32[256]{0:T(256)} %param.15) | copy-start | bytes 3076
where the time goes:
time: 748 us; the launch traced here: 746 us
  local copies, waits for them, and re-layouts  637 us (85%)
  matrix products  69.8 us (9%)
  starting transfers between devices  18.6 us (2%)
  other arithmetic  11 us (1%)
  waiting for transfers between devices  10 us (1%)
    gather x4, local copies, waits for them, and re-layouts, point_value(): jnp.take_along_axis(source, jnp.clip(index, 0, last_slot), axis=-1)  550 us
    conv_general_dilated x4, local copies, waits for them, and re-layouts, second_layer(): lax.conv_general_dilated(hidden[None], kernel, (1, 1), 'VALID', rhs_dilat...  48 us
    conv_general_dilated x1, matrix products, first_layer(): lax.conv_general_dilated(padded[None, None], kernel, (1, 1), 'VALID', rhs...  38.4 us
    conv_general_dilated x1, matrix products, second_layer(): lax.conv_general_dilated(hidden[None], kernel, (1, 1), 'VALID', rhs_dilat...  31.4 us
    squeeze x1, local copies, waits for them, and re-layouts, second_layer(): lax.conv_general_dilated(hidden[None], kernel, (1, 1), 'VALID', rhs_dilat...  16.1 us
  transfers between devices with their start and end apart: 7, of which 5 were waited for; matrix products, arithmetic and copies ran while one was open for 74% of the time, Pallas kernels for 0%

commit v1 on v0

v1 whole, which is shorter than its diff:
```python
import functools
import math

import jax
import jax.numpy as jnp
from jax import lax
from jax.experimental import pallas as pl
from jax.experimental.pallas import tpu as pltpu
from jax.sharding import PartitionSpec as P

Q = 2048
GROUPS = 8
D1 = 2
D2 = 8
F32 = jnp.float32
BF16 = jnp.bfloat16
RE = 40
TILES = 9
WID = TILES * 128
GA = math.sqrt(2.0 / math.pi)
GB = GA * 0.044715


def gelu2(v):
    t = jnp.tanh(v * (v * v * GB + GA))
    return v + v * t


def candidates(u):
    if u == 8:
        return [-1, 0, 12, 13, 14, 15, 16]
    low = math.floor(1.501 * u - 0.008)
    high = 2 * u + 2
    cands = [c for c in range(low, min(high, 15) + 1)]
    if u == 7:
        cands.append(16)
    return cands


def regrid(src, lens, offs, parity, u):
    lane = lax.broadcasted_iota(jnp.int32, (RE, 128), 1)
    m = u * 128 + lane
    if u == 8:
        m = jnp.where(lane >= 64, m - WID, m)
    j = 2 * m + parity
    num = (2 * j + 1) * lens - 2048 - 1024 * offs
    low = num >> 12
    frac = (num & 4095).astype(F32) * (1.0 / 4096.0)
    cands = candidates(u)

    def value(e):
        over = e >= lens
        if 16 in cands:
            past = e - lens
            blk = jnp.where(over, 16, e >> 7)
            idx = jnp.where(over, past, e) & 127
        else:
            blk = e >> 7
            idx = e & 127
        result = None
        for c in cands:
            got = jnp.take_along_axis(src(c), idx, axis=1)
            result = got if result is None else jnp.where(blk == c, got, result)
        return result

    return (1.0 - frac) * value(low) + frac * value(low + 1)


def compute_kernel(t_ref, src_ref, len_ref, off_ref, w1_ref, b1_ref, w2_ref, b2_ref, out_ref, x_ref, band_ref, wide_ref, hid_ref, shift_ref, acc_ref):
    tile = t_ref[0]
    row = lax.broadcasted_iota(jnp.int32, (RE, 128), 0)
    globe = row + tile * 16 - 10
    kept = (globe >= 0) & (globe < 256) & (row < 36)
    lens = len_ref[...]
    offs = off_ref[...]

    lane = lax.broadcasted_iota(jnp.int32, (32, 128), 1)
    taps = w1_ref[...].astype(F32)
    bias = b1_ref[...]
    b_hi = bias.astype(BF16).astype(F32)
    b_mid = (bias - b_hi).astype(BF16).astype(F32)
    b_lo = bias - b_hi - b_mid
    zero = jnp.zeros((32, 128), F32)
    tail = jnp.where(lane == 120, b_hi, jnp.where(lane == 121, b_mid, jnp.where(lane == 122, b_lo, zero)))
    tap_w = [jnp.broadcast_to(taps[:, k : k + 1], (32, 128)) for k in range(9)]
    for p in range(4):
        for q in range(2):
            for a2 in range(4):
                r = 2 * p + q + 8 * a2
                full = tail
                for a in range(3):
                    for b in range(3):
                        full = jnp.where(lane == b * RE + r + 2 * a, tap_w[3 * a + b], full)
                band_ref[pl.ds(((p * 2 + q) * 4 + a2) * 32, 32), :] = full.astype(BF16)

    w2 = w2_ref[...].astype(F32) * 0.5
    gap = jnp.zeros((64, 96), F32)
    wide = jnp.concatenate([jnp.concatenate([w2, gap], axis=1), jnp.concatenate([gap, w2], axis=1)], axis=0)
    k = lax.broadcasted_iota(jnp.int32, (128, 384), 1)
    dead = ((tile == 0) & (k < 96)) | ((tile == 15) & (k >= 288))
    wide_ref[...] = jnp.where(dead, 0.0, wide).astype(BF16)
    b2 = b2_ref[...]

    def src(c):
        return src_ref[:, pl.ds((c + 1) * 128, 128)].astype(F32)

    ones = jnp.ones((8, 128), F32)
    zlane = lax.broadcasted_iota(jnp.int32, (RE, 128), 1)
    for parity in range(2):
        reg = [jnp.where(kept, regrid(src, lens, offs, parity, u), 0.0) for u in range(TILES)]
        for u in range(TILES):
            before, after = reg[u - 1], reg[(u + 1) % TILES]
            left = jnp.where(zlane < 1, pltpu.roll(before, 1, 1), pltpu.roll(reg[u], 1, 1))
            right = jnp.where(zlane >= 127, pltpu.roll(after, 127, 1), pltpu.roll(reg[u], 127, 1))
            x_ref[parity, :, pl.ds(u * 128, 128)] = jnp.concatenate([left, reg[u], right, ones], axis=0).astype(BF16)

    hlane = lax.broadcasted_iota(jnp.int32, (256, 128), 1)

    def step(p, carry):
        band = band_ref[pl.ds(pl.multiple_of(p * 256, 256), 256), :]
        for parity in range(2):
            for u in range(TILES):
                pre = jnp.dot(band, x_ref[parity, :, pl.ds(u * 128, 128)], preferred_element_type=F32)
                hid_ref[parity, :, pl.ds(u * 128, 128)] = gelu2(pre).astype(BF16)
        for parity in range(2):
            for u in range(8):
                mid = hid_ref[parity, :, pl.ds(u * 128, 128)]
                before = hid_ref[parity, :, pl.ds(((u - 1) % TILES) * 128, 128)]
                after = hid_ref[parity, :, pl.ds((u + 1) * 128, 128)]
                left = jnp.concatenate([before[:, 124:], mid[:, :124]], axis=1)
                right = jnp.concatenate([mid[:, 4:], after[:, :4]], axis=1)
                for q in range(2):
                    for a2 in range(4):
                        rows = slice((q * 4 + a2) * 32, (q * 4 + a2 + 1) * 32)
                        for b, part in enumerate((left, mid, right)):
                            shift_ref[parity, pl.ds(q * 384 + (a2 * 3 + b) * 32, 32), pl.ds(u * 128, 128)] = part[rows]
        wide = wide_ref[...]
        for u in range(4):
            cols = pl.ds(u * 256, 256)
            total = None
            for parity in range(2):
                for q in range(2):
                    pre = jnp.dot(wide, shift_ref[parity, pl.ds(q * 384, 384), cols], preferred_element_type=F32)
                    one = gelu2(pre + b2)
                    total = one if total is None else total + one
            total = total * 0.125
            for w in range(2):
                lanes = slice(w * 128, (w + 1) * 128)
                base = (2 * u + w) * 512
                acc_ref[pl.ds(pl.multiple_of(base + p * 64, 64), 64), :] = total[:64, lanes]
                acc_ref[pl.ds(pl.multiple_of(base + p * 64 + 256, 64), 64), :] = total[64:, lanes]
        return carry

    lax.fori_loop(0, 4, step, 0)
    for o in range(64):
        out_ref[o] = jnp.concatenate([acc_ref[pl.ds(u * 512 + o, 8, stride=64), :] for u in range(8)], axis=1).astype(BF16)


def compute(tile, src, lens, offs, w1, b1, w2, b2):
    smem = pl.BlockSpec(memory_space=pltpu.SMEM)
    vmem = pl.BlockSpec(memory_space=pltpu.VMEM)
    return pl.pallas_call(
        compute_kernel,
        out_shape=jax.ShapeDtypeStruct((64, 8, 1024), BF16),
        in_specs=[smem] + [vmem] * 7,
        out_specs=vmem,
        scratch_shapes=[
            pltpu.VMEM((2, 128, WID), BF16),
            pltpu.VMEM((1024, 128), BF16),
            pltpu.VMEM((128, 384), BF16),
            pltpu.VMEM((2, 256, WID), BF16),
            pltpu.VMEM((2, 768, 1024), BF16),
            pltpu.VMEM((4096, 128), F32),
        ],
        compiler_params=pltpu.CompilerParams(vmem_limit_bytes=48 << 20),
    )(tile, src, lens, offs, w1, b1, w2, b2)


def with_halo(block, sides, width):
    for axis, dim in sides:
        count = lax.axis_size(axis)
        forward = [(i, i + 1) for i in range(count - 1)]
        forward.append((count - 1, 0))
        backward = [(target, source) for source, target in forward]
        low = lax.ppermute(
            lax.slice_in_dim(block, block.shape[dim] - width, None, axis=dim), axis, forward
        )
        high = lax.ppermute(lax.slice_in_dim(block, 0, width, axis=dim), axis, backward)
        block = jnp.concatenate([low, block, high], axis=dim)
    return block


def pack_rows(values, stored_row, lat_index, band_count, capacity):
    row_count = values.shape[0]
    held_ids = lax.dynamic_slice_in_dim(stored_row, lat_index * row_count, row_count)
    tile_of = held_ids // row_count
    one_hot = (tile_of[:, None] == jnp.arange(band_count, dtype=jnp.int32)[None, :]).astype(
        jnp.int32
    )
    rank_of = jnp.sum((jnp.cumsum(one_hot, axis=0) - 1) * one_hot, axis=1)
    slot_of = tile_of * capacity + rank_of
    buffer = (
        jnp.zeros((band_count * capacity, values.shape[1]), values.dtype).at[slot_of].set(values)
    )
    return buffer.reshape(band_count, capacity, values.shape[1])


def unpack_rows(arrived, stored_row, lat_index, row_count, band_count, capacity):
    held_all = stored_row.reshape(band_count, row_count)
    tile_of = held_all // row_count
    one_hot = (
        tile_of[:, :, None] == jnp.arange(band_count, dtype=jnp.int32)[None, None, :]
    ).astype(jnp.int32)
    rank_of = jnp.sum((jnp.cumsum(one_hot, axis=1) - 1) * one_hot, axis=2)
    slot_of = jnp.arange(band_count, dtype=jnp.int32)[:, None] * capacity + rank_of
    is_mine = tile_of == lat_index
    target = jnp.where(is_mine, held_all % row_count, row_count)
    source = (
        jnp.zeros((row_count,), jnp.int32)
        .at[target.reshape(-1)]
        .set(slot_of.reshape(-1), mode="drop")
    )
    flat_rows = arrived.reshape(band_count * capacity, arrived.shape[2])
    return jnp.take(flat_rows, source, axis=0)


def per_device(field, stored_row, row_len, offset, first_weight, first_bias, second_weight, second_bias):
    row_count = field.shape[0]
    band_count = lax.axis_size("lat")
    lat_index = lax.axis_index("lat")
    bundle = pack_rows(field, stored_row, lat_index, band_count, row_count // GROUPS)
    arrived = lax.all_to_all(bundle, "lat", split_axis=0, concat_axis=0, tiled=True)
    rows = unpack_rows(arrived, stored_row, lat_index, row_count, band_count, row_count // GROUPS)
    rows = with_halo(rows, (("lat", 0),), D1 + D2)
    ids = jnp.clip(lat_index * row_count - D1 - D2 + jnp.arange(RE, dtype=jnp.int32), 0, 255)
    lens = jnp.take(row_len, ids)
    offs = jnp.take(offset, ids)
    rows = jnp.pad(rows, ((0, RE - rows.shape[0]), (0, 0)))
    tail = jnp.take_along_axis(rows, lens[:, None] - 16 + jnp.arange(16, dtype=jnp.int32)[None, :], axis=1)
    count = lax.axis_size("lon")
    forward = [(i, (i + 1) % count) for i in range(count)]
    backward = [((i + 1) % count, i) for i in range(count)]
    before = lax.ppermute(tail, "lon", forward)
    after = lax.ppermute(rows[:, :16], "lon", backward)
    src = jnp.concatenate([jnp.pad(before, ((0, 0), (112, 0))), rows, jnp.pad(after, ((0, 0), (0, 112)))], axis=1)
    spread = lambda v: jnp.broadcast_to(v[:, None], (RE, 128))
    return compute(
        lat_index[None].astype(jnp.int32),
        src,
        spread(lens),
        spread(offs),
        first_weight,
        first_bias[:, None],
        second_weight,
        jnp.concatenate([second_bias, second_bias])[:, None],
    )


def solution(mesh):
    placed = (P("lat", "lon"), P(), P(), P(), P(), P(), P(), P())
    return jax.shard_map(
        per_device, mesh=mesh, in_specs=placed, out_specs=P(None, "lat", "lon"), check_vma=False
    )
```

time: 748 us -> 57.2 us (0.08)
  the two profiles are of different devices: /device:TPU:1 before, /device:TPU:0 now
where the time goes in v1:
time: 57.2 us; the launch traced here: 56.9 us
  starting transfers between devices  15.9 us (28%)
  local copies, waits for them, and re-layouts  14.7 us (26%)
  Pallas kernels  14.7 us (26%)
  waiting for transfers between devices  9.93 us (17%)
  other arithmetic  1.44 us (3%)
    pallas_call x1, Pallas kernels, compute(): pl.pallas_call(compute_kernel, out_shape=jax.ShapeDtypeStruct((64, 8, 102...  14.7 us
    ppermute x1, starting transfers between devices, per_device(): after = lax.ppermute(rows[:, :16], 'lon', backward)  6.44 us
    gather x3, local copies, waits for them, and re-layouts, per_device(): jnp.take_along_axis(rows, lens[:, None] - 16 + jnp.arange(16, dtype=jnp.i...  5.92 us
    ppermute x1, waiting for transfers between devices, per_device(): before = lax.ppermute(tail, 'lon', forward)  5.9 us
    all_to_all x1, starting transfers between devices, per_device(): lax.all_to_all(bundle, 'lat', split_axis=0, concat_axis=0, tiled=True)  5.5 us
    ppermute x1, starting transfers between devices, with_halo(): lax.ppermute(lax.slice_in_dim(block, 0, width, axis=dim), axis, backward)  3.73 us
    unnamed x15, local copies, waits for them, and re-layouts  2.7 us
    ppermute x1, waiting for transfers between devices, with_halo(): lax.ppermute(lax.slice_in_dim(block, block.shape[dim] - width, None, axis...  1.86 us
  transfers between devices with their start and end apart: 5, of which 4 were waited for; matrix products, arithmetic and copies ran while one was open for 8% of the time, Pallas kernels for 0%

profile of v1, /device:TPU:0, one launch (start us, length us, event | category | flops | bytes accessed | tf_op | source)
XLA Modules:
  0.0 56.9 jit_solution(7534232658681800522)
XLA Ops:
  0.0 0.0 copy-start
  0.0 0.7 %copy-done.3 = s32[256]{0:T(256)S(1)} copy-done((s32[256]{0:T(256)S(1)}, s32[256]{0:T(256)}, u32[]{:S(2)}) %copy-start.3) | copy-done | bytes 1048
  0.7 0.1 and_select_fusion
  0.8 0.1 fusion.22
  0.9 0.2 select_reduce_fusion
  1.1 0.1 compare_select_fusion.4
  1.2 1.1 %scatter_custom_fusion.1 = bf16[32,2048]{1,0:T(8,128)(2,1)S(1)} fusion(s32[16]{0:T(128)S(1)} %compare_select_fusion.4, bf16[16,2048]{1,0:T(8,128)(2,1)} %param.10, bf16[]{:T(256)} %constant.115.clone.1), kind=kCustom, calls=%fused_computation.22 | custom fusion | bytes 131584 | tf_op jit(solution)/shard_map/scatter | solution.py:203
  2.2 0.8 %reshape.120 = bf16[16,2,2048]{2,1,0:T(2,128)(2,1)} reshape(bf16[32,2048]{1,0:T(8,128)(2,1)S(1)} %scatter_custom_fusion.1) | data formatting | bytes 262144 | tf_op jit(solution)/shard_map/reshape | solution.py:205
  3.0 5.5 %all-to-all-start = ((bf16[16,2,2048]{2,1,0:T(2,128)(2,1)}), bf16[16,2,2048]{2,1,0:T(2,128)(2,1)S(1)}, u32[]{:S(2)}, u32[]{:S(2)}) async-start(bf16[16,2,2048]{2,1,0:T(2,128)(2,1)} %reshape.120), calls=%async_computation | async-start | bytes 262144 | tf_op jit(solution)/shard_map/all_to_all | solution.py:232
  8.5 0.1 reshape.119
  8.6 0.8 %gather_fusion.2 = s32[40]{0:T(128)S(1)} fusion(s32[256]{0:T(256)S(1)} %copy-done, s32[1024]{0:T(1024)S(1)} %pad_clamp_fusion.1), kind=kCustom, calls=%fused_computation.clone | custom fusion | bytes 480 | tf_op jit(solution)/shard_map/jit(_take)/gather | solution.py:236
  9.4 0.1 copy.21
  9.5 0.5 fusion.27
  10.0 0.1 copy.22
  10.1 0.1 reshape.156
  10.1 1.4 %scatter_custom_fusion = s32[16]{0:T(128)S(1)} fusion(s32[256]{0:T(256)S(1)} %compare_select_fusion.2, s32[256]{0:T(256)S(1)} %reshape.156, s32[]{:T(128)} %constant.101.clone.1), kind=kCustom, calls=%fused_computation.68 | custom fusion | bytes 68 | tf_op jit(solution)/shard_map/scatter | solution.py:221
  11.6 0.1 fusion.16
  11.6 0.0 copy-start.2
  11.7 0.7 %copy-done.2 = s32[256]{0:T(256)S(1)} copy-done((s32[256]{0:T(256)S(1)}, s32[256]{0:T(256)}, u32[]{:S(2)}) %copy-start.2) | copy-done | bytes 1048
  12.3 0.8 %gather_fusion.3 = s32[40]{0:T(128)S(1)} fusion(s32[256]{0:T(256)S(1)} %copy-done.2, s32[1024]{0:T(1024)S(1)} %pad_clamp_fusion.1), kind=kCustom, calls=%fused_computation.1.clone | custom fusion | bytes 480 | tf_op jit(solution)/shard_map/jit(_take)/gather | solution.py:237
  13.1 1.8 %all-to-all-done = bf16[16,2,2048]{2,1,0:T(2,128)(2,1)S(1)} async-done(((bf16[16,2,2048]{2,1,0:T(2,128)(2,1)}), bf16[16,2,2048]{2,1,0:T(2,128)(2,1)S(1)}, u32[]{:S(2)}, u32[]{:S(2)}) %all-to-all-start) | async-done | bytes 131104 | tf_op jit(solution)/shard_map/all_to_all | solution.py:232
  14.9 0.1 reshape.121
  15.0 0.6 %gather_fusion = bf16[16,2048]{1,0:T(8,128)(2,1)S(1)} fusion(bf16[32,2048]{1,0:T(8,128)(2,1)S(1)} %reshape.121, s32[1024]{0:T(1024)S(1)} %pad_clamp_fusion), kind=kCustom, calls=%fused_computation.2 | custom fusion | bytes 131136 | tf_op jit(solution)/shard_map/jit(_take)/gather | solution.py:224
  15.6 0.1 broadcast_select_fusion
  15.7 0.2 collective-permute-start
  15.9 3.7 %collective-permute-start.1 = (bf16[10,2048]{1,0:T(8,128)(2,1)S(1)}, bf16[10,2048]{1,0:T(8,128)(2,1)S(1)}, u32[]{:S(2)}, u32[]{:S(2)}) collective-permute-start(bf16[10,2048]{1,0:T(8,128)(2,1)S(1)} %get-tuple-element.9), channel_id=1, source_target_pairs={{8,0},{16,8},{24,16},{32,24},{40,32},{48,40},{56,48},{64,56},{72,6... | collective-permute-start | bytes 122888 | tf_op jit(solution)/shard_map/ppermute | solution.py:188
  19.6 0.1 reshape.146
  19.7 1.9 %collective-permute-done = bf16[10,2048]{1,0:T(8,128)(2,1)S(1)} collective-permute-done((bf16[10,2048]{1,0:T(8,128)(2,1)S(1)}, bf16[10,2048]{1,0:T(8,128)(2,1)S(1)}, u32[]{:S(2)}, u32[]{:S(2)}) %collective-permute-start) | collective-permute-done | bytes 40992 | tf_op jit(solution)/shard_map/ppermute | solution.py:185
  21.6 0.0 collective-permute-done.1
  21.6 0.1 fusion.9
  21.7 5.8 %gather_fusion.1 = bf16[640]{0:T(1024)(128)(2,1)S(1)} fusion(bf16[40,2048]{1,0:T(8,128)(2,1)S(1)} %fusion.9, s32[640]{0:T(1024)S(1)} %reshape.146), kind=kCustom, calls=%fused_computation.3 | custom fusion | bytes 7680 | tf_op jit(solution)/shard_map/jit(take_along_axis)/gather | solution.py:239
  27.4 0.1 reshape.149
  27.5 0.0 copy-start.4
  27.5 0.1 fusion.20
  27.6 6.4 %collective-permute-start.3 = (bf16[40,16]{1,0:T(8,128)(2,1)S(1)}, bf16[40,16]{1,0:T(8,128)(2,1)S(1)}, u32[]{:S(2)}, u32[]{:S(2)}) collective-permute-start(bf16[40,16]{1,0:T(8,128)(2,1)S(1)} %slice.22), channel_id=1, source_target_pairs={{1,0},{2,1},{3,2},{4,3},{5,4},{6,5},{7,6},{0,7},{9,8},{10,9},{11,1... | collective-permute-start | bytes 3848 | tf_op jit(solution)/shard_map/ppermute | solution.py:244
  34.0 0.0 collective-permute-start.2
  34.0 0.1 maximum_bitcast_fusion
  34.1 0.1 copy.23.w1_ref
  34.2 0.7 %copy-done.5 = f32[32]{0:T(128)S(1)} copy-done((f32[32]{0:T(128)S(1)}, f32[32]{0:T(128)}, u32[]{:S(2)}) %copy-start.5) | copy-done | bytes 152
  34.9 0.1 copy.24.b1_ref
  35.0 0.1 copy.25.b2_ref
  35.1 0.3 collective-permute-done.3
  35.4 5.9 %collective-permute-done.2 = bf16[40,16]{1,0:T(8,128)(2,1)S(1)} collective-permute-done((bf16[40,16]{1,0:T(8,128)(2,1)S(1)}, bf16[40,16]{1,0:T(8,128)(2,1)S(1)}, u32[]{:S(2)}, u32[]{:S(2)}) %collective-permute-start.2) | collective-permute-done | bytes 1312 | tf_op jit(solution)/shard_map/ppermute | solution.py:243
  41.3 0.1 fusion.6.src_ref
  41.4 0.1 broadcast_in_dim.69.len_ref
  41.5 0.1 broadcast_in_dim.70.off_ref
  41.6 0.6 %copy-done.1 = bf16[64,288]{1,0:T(8,128)(2,1)S(1)} copy-done((bf16[64,288]{1,0:T(8,128)(2,1)S(1)}, bf16[64,288]{1,0:T(8,128)(2,1)}, u32[]{:S(2)}) %copy-start.1) | copy-done | bytes 36888
  42.1 14.7 %shard_map.82 = bf16[64,8,1024]{2,1,0:T(8,128)(2,1)} custom-call(s32[1]{0:T(128)} %bitcast.t_ref, bf16[40,2304]{1,0:T(8,128)(2,1)S(1)} %fusion.6.src_ref, s32[40,128]{1,0:T(8,128)S(1)} %broadcast_in_dim.69.len_ref, s32[40,128]{1,0:T(8,128)S(1)} %broadcast_in_dim.70.off_ref, bf16[32,9]{1,0:T(8,128)(2,1)S(1)} %copy.23.w1_ref, f32[32,1]{1,0:T(8,128)S(1)} %copy.24.b1_ref, ...), custom_call_target="tpu_custom_call" | custom-call | tf_op jit(solution)/shard_map/pallas_call | solution.py:162
  (21 shorter events, 0.2 us)
Async XLA Ops:
  0.0 8.6 %copy-start = (s32[256]{0:T(256)S(1)}, s32[256]{0:T(256)}, u32[]{:S(2)}) copy-start(s32[256]{0:T(256)} %param.12) | copy-start | bytes 3076
  0.0 0.7 %copy-start.3 = (s32[256]{0:T(256)S(1)}, s32[256]{0:T(256)}, u32[]{:S(2)}) copy-start(s32[256]{0:T(256)} %param.11) | copy-start | bytes 3076
  3.0 12.0 %all-to-all-start = ((bf16[16,2,2048]{2,1,0:T(2,128)(2,1)}), bf16[16,2,2048]{2,1,0:T(2,128)(2,1)S(1)}, u32[]{:S(2)}, u32[]{:S(2)}) async-start(bf16[16,2,2048]{2,1,0:T(2,128)(2,1)} %reshape.120), calls=%async_computation | async-start | bytes 262144 | tf_op jit(solution)/shard_map/all_to_all | solution.py:232
  11.6 0.7 %copy-start.2 = (s32[256]{0:T(256)S(1)}, s32[256]{0:T(256)}, u32[]{:S(2)}) copy-start(s32[256]{0:T(256)} %param.13) | copy-start | bytes 3076
  15.7 5.9 %collective-permute-start = (bf16[10,2048]{1,0:T(8,128)(2,1)S(1)}, bf16[10,2048]{1,0:T(8,128)(2,1)S(1)}, u32[]{:S(2)}, u32[]{:S(2)}) collective-permute-start(bf16[10,2048]{1,0:T(8,128)(2,1)S(1)} %get-tuple-element.8), channel_id=1, source_target_pairs={{0,8},{8,16},{16,24},{24,32},{32,40},{40,48},{48,56},{56,64},{64,7... | collective-permute-start | bytes 122888 | tf_op jit(solution)/shard_map/ppermute | solution.py:185
  15.9 5.7 %collective-permute-start.1 = (bf16[10,2048]{1,0:T(8,128)(2,1)S(1)}, bf16[10,2048]{1,0:T(8,128)(2,1)S(1)}, u32[]{:S(2)}, u32[]{:S(2)}) collective-permute-start(bf16[10,2048]{1,0:T(8,128)(2,1)S(1)} %get-tuple-element.9), channel_id=1, source_target_pairs={{8,0},{16,8},{24,16},{32,24},{40,32},{48,40},{56,48},{64,56},{72,6... | collective-permute-start | bytes 122888 | tf_op jit(solution)/shard_map/ppermute | solution.py:188
  27.5 6.5 %copy-start.6 = (f32[64]{0:T(128)S(1)}, f32[64]{0:T(128)}, u32[]{:S(2)}) copy-start(f32[64]{0:T(128)} %param.17) | copy-start | bytes 772
  27.5 6.6 %copy-start.4 = (bf16[32,9]{0,1:T(8,128)(2,1)S(1)}, bf16[32,9]{0,1:T(8,128)(2,1)}, u32[]{:S(2)}) copy-start(bf16[32,9]{0,1:T(8,128)(2,1)} %param.14) | copy-start | bytes 1732
  27.6 7.8 %collective-permute-start.3 = (bf16[40,16]{1,0:T(8,128)(2,1)S(1)}, bf16[40,16]{1,0:T(8,128)(2,1)S(1)}, u32[]{:S(2)}, u32[]{:S(2)}) collective-permute-start(bf16[40,16]{1,0:T(8,128)(2,1)S(1)} %slice.22), channel_id=1, source_target_pairs={{1,0},{2,1},{3,2},{4,3},{5,4},{6,5},{7,6},{0,7},{9,8},{10,9},{11,1... | collective-permute-start | bytes 3848 | tf_op jit(solution)/shard_map/ppermute | solution.py:244
  34.0 7.3 %collective-permute-start.2 = (bf16[40,16]{1,0:T(8,128)(2,1)S(1)}, bf16[40,16]{1,0:T(8,128)(2,1)S(1)}, u32[]{:S(2)}, u32[]{:S(2)}) collective-permute-start(bf16[40,16]{1,0:T(8,128)(2,1)S(1)} %fusion.20), channel_id=1, source_target_pairs={{0,1},{1,2},{2,3},{3,4},{4,5},{5,6},{6,7},{7,0},{8,9},{9,10},{10,1... | collective-permute-start | bytes 3848 | tf_op jit(solution)/shard_map/ppermute | solution.py:243
  34.2 0.7 %copy-start.5 = (f32[32]{0:T(128)S(1)}, f32[32]{0:T(128)}, u32[]{:S(2)}) copy-start(f32[32]{0:T(128)} %param.15) | copy-start | bytes 388
  41.3 0.8 %copy-start.1 = (bf16[64,288]{1,0:T(8,128)(2,1)S(1)}, bf16[64,288]{1,0:T(8,128)(2,1)}, u32[]{:S(2)}) copy-start(bf16[64,288]{1,0:T(8,128)(2,1)} %w2_ref.1) | copy-start | bytes 110596
